TPU v7x, 256 devices: a whole 4x4x8 slice. The times are simulated.
256 devices in a mesh: dp: 8 (over y, core), space: 32 (over z, x).
Axes of the slice: x: 4, y: 4, z: 8, core: 2. Of those that a mesh axis runs over, the one named last changes fastest.
Arguments:
- features: bfloat16 [8, 64, 64, 256], P('dp', None, 'space'), may hold values from -6 to 6
- kernel_a: bfloat16 [27, 64, 128], replicated, may hold values from -0.15625 to 0.15625
- kernel_b: bfloat16 [27, 128, 256], replicated, may hold values from -0.109375 to 0.109375
- upstream: bfloat16 [8, 256, 32, 64], P('dp', None, 'space'), may hold values from -24 to 24
Outputs:
- grad_input: bfloat16 [8, 64, 64, 256], P('dp', None, 'space')
- grad_kernel_a: float32 [27, 64, 128], replicated
- grad_kernel_b: float32 [27, 128, 256], P(None, None, 'space')
All inputs are finite; a program needn't handle non-finite values.
Results may differ from a plain program's by a relative error of at most 0.0075.
Values may be sent and summed in bfloat16 or wider, within the bound.
A program may use at most 64 MiB of HBM per device.

v0:
```python
import math
import jax
import jax.numpy as jnp
from jax import lax
from jax.sharding import PartitionSpec as P

GY = 16
GZ = 16


def with_halo(value, sides, width):
    for axis, dim in sides:
        count, length = (lax.axis_size(axis), value.shape[dim])
        up = [(i, (i + 1) % count) for i in range(count - 1)]
        down = [(j, i) for i, j in up]
        last = lax.slice_in_dim(value, length - width, length, axis=dim)
        leading = lax.slice_in_dim(value, 0, width, axis=dim)
        before = lax.ppermute(last, axis, up)
        after = lax.ppermute(leading, axis, down)
        value = jnp.concatenate([before, value, after], axis=dim)
    return value


def tap_view(padded_flat, off_x, off_y, off_z, planes, span_z, cell_count, column):
    shift_z = off_z - 1
    keep_mask = ((column + shift_z >= 0) & (column + shift_z < span_z)).astype(padded_flat.dtype)
    begin = off_y * span_z + off_z
    return padded_flat[:, :, off_x : off_x + planes, begin : begin + cell_count] * keep_mask


def pad_cells(source, span_z):
    return jnp.pad(source, ((0, 0), (0, 0), (0, 0), (span_z + 1, span_z + 1)))


def pad_planes(source):
    return jnp.pad(source, ((0, 0), (0, 0), (1, 1), (0, 0)))


def conv_forward(rimmed, kernel, planes, span_y, span_z):
    cell_count = span_y * span_z
    padded_flat = pad_cells(rimmed, span_z)
    column = lax.broadcasted_iota(jnp.int32, (cell_count,), 0) % span_z
    summed = None
    for tap_index in range(27):
        shifted = tap_view(
            padded_flat,
            tap_index // 9,
            tap_index // 3 % 3,
            tap_index % 3,
            planes,
            span_z,
            cell_count,
            column,
        )
        product = jnp.einsum(
            "io,sixn->soxn", kernel[tap_index], shifted, preferred_element_type=jnp.float32
        )
        summed = product if summed is None else summed + product
    return summed


def conv_transposed(rimmed, kernel, planes, span_y, span_z):
    cell_count = span_y * span_z
    padded_flat = pad_cells(rimmed, span_z)
    column = lax.broadcasted_iota(jnp.int32, (cell_count,), 0) % span_z
    summed = None
    for tap_index in range(27):
        shifted = tap_view(
            padded_flat,
            2 - tap_index // 9,
            2 - tap_index // 3 % 3,
            2 - tap_index % 3,
            planes,
            span_z,
            cell_count,
            column,
        )
        product = jnp.einsum(
            "io,soxn->sixn", kernel[tap_index], shifted, preferred_element_type=jnp.float32
        )
        summed = product if summed is None else summed + product
    return summed


def kernel_grad(rimmed, gradient, planes, span_y, span_z):
    cell_count = span_y * span_z
    padded_flat = pad_cells(rimmed, span_z)
    column = lax.broadcasted_iota(jnp.int32, (cell_count,), 0) % span_z
    terms = []
    for tap_index in range(27):
        shifted = tap_view(
            padded_flat,
            tap_index // 9,
            tap_index // 3 % 3,
            tap_index % 3,
            planes,
            span_z,
            cell_count,
            column,
        )
        terms.append(
            jnp.einsum("sixn,soxn->io", shifted, gradient, preferred_element_type=jnp.float32)
        )
    return jnp.stack(terms)


def silu_slope(value):
    sigma = jax.nn.sigmoid(value)
    return sigma * (1.0 + value * (1.0 - sigma))


def body(features, kernel_a, kernel_b, upstream):
    samples = features.shape[0]
    planes = features.shape[2]
    half_planes = planes // 2
    half_y, half_z = (GY // 2, GZ // 2)
    rimmed_in = with_halo(features, (("space", 2),), 1)
    pre_a = conv_forward(rimmed_in, kernel_a, planes, GY, GZ)
    filters_a = pre_a.shape[1]
    pooled = (
        jax.nn.silu(pre_a)
        .reshape(samples, filters_a, half_planes, 2, half_y, 2, half_z, 2)
        .mean(axis=(3, 5, 7))
    )
    pooled = pooled.reshape(samples, filters_a, half_planes, half_y * half_z).astype(jnp.bfloat16)
    per_device = kernel_b.shape[2] // lax.axis_size("space")
    gathered = lax.all_gather(pooled, "space", axis=2, tiled=True)
    full_planes = gathered.shape[2]
    own_kernel = lax.dynamic_slice_in_dim(
        kernel_b, lax.axis_index("space") * per_device, per_device, 2
    )
    padded_pooled = pad_planes(gathered)
    pre_b = conv_forward(padded_pooled, own_kernel, full_planes, half_y, half_z)
    upstream_own = lax.all_to_all(upstream, "space", split_axis=1, concat_axis=2, tiled=True)
    grad_pre_b = (upstream_own.astype(jnp.float32) * silu_slope(pre_b)).astype(jnp.bfloat16)
    part_b = kernel_grad(padded_pooled, grad_pre_b, full_planes, half_y, half_z)
    padded_grad = pad_planes(grad_pre_b)
    term_rows = conv_transposed(
        padded_grad, own_kernel, half_planes * lax.axis_size("space"), half_y, half_z
    )
    own_rows = lax.psum_scatter(
        jnp.transpose(term_rows, (2, 0, 1, 3)), "space", scatter_dimension=0, tiled=True
    )
    grad_pool = jnp.transpose(own_rows, (1, 2, 0, 3))
    samples_all = samples * lax.axis_size("dp")
    cells_all = planes * lax.axis_size("space") * GY * GZ
    scale_a = 1.0 / math.sqrt(samples_all * cells_all)
    scale_b = 1.0 / math.sqrt(samples_all * cells_all / 8)
    grad_kernel_b = lax.psum(part_b, "dp") * scale_b
    spread = jnp.broadcast_to(
        grad_pool.reshape(samples, filters_a, half_planes, 1, half_y, 1, half_z, 1),
        (samples, filters_a, half_planes, 2, half_y, 2, half_z, 2),
    )
    spread = spread.reshape(samples, filters_a, planes, GY * GZ)
    grad_pre_a = (spread * 0.125 * silu_slope(pre_a)).astype(jnp.bfloat16)
    part_a = kernel_grad(rimmed_in, grad_pre_a, planes, GY, GZ)
    grad_kernel_a = lax.psum(part_a, ("dp", "space")) * scale_a
    rimmed_back = with_halo(grad_pre_a, (("space", 2),), 1)
    grad_input = conv_transposed(rimmed_back, kernel_a, planes, GY, GZ).astype(jnp.bfloat16)
    return (grad_input, grad_kernel_a, grad_kernel_b)


def solution(mesh):
    return jax.shard_map(
        body,
        mesh=mesh,
        in_specs=(P("dp", None, "space", None), P(), P(), P("dp", None, "space", None)),
        out_specs=(P("dp", None, "space", None), P(), P(None, None, "space")),
        check_vma=False,
    )
```

profile of v0, /device:TPU:1, one launch (start us, length us, event | category | flops | bytes accessed | tf_op | source)
XLA Modules:
  0.0 672.9 jit_solution(3354463360023690337)
XLA Ops:
  8.0 1.1 fusion.850
  9.1 3.9 collective-permute-start
  13.1 1.3 collective-permute-start.1
  15.8 1.0 reduce.3
  17.5 12.8 %all-to-all-start = ((bf16[32,2,256]{2,1,0:T(2,128)(2,1)}), bf16[32,2,256]{2,1,0:T(2,128)(2,1)S(1)}, u32[]{:S(2)}, u32[]{:S(2)}) async-start(bf16[32,2,256]{2,1,0:T(2,128)(2,1)} %reshape.962), calls=%async_computation | async-start | bytes 65536 | tf_op jit(solution)/shard_map/all_to_all | solution.py:134
  30.5 1.5 select_maximum_fusion
  32.0 1.0 fusion.373
  33.1 1.5 fusion.371
  41.2 1.0 multiply_reduce_fusion
  42.4 38.8 %all_gather.3 = bf16[1,128,32,64]{1,3,0,2:T(8,128)(2,1)S(1)} all-gather(bf16[1,128,1,64]{1,3,0,2:T(8,128)(2,1)S(1)} %fusion.606), channel_id=1, replica_groups=mesh['dp'=8,'space'=32] {'space'}, dimensions={2}, use_global_device_ids=true | all-gather | bytes 540672 | tf_op jit(solution)/shard_map/all_gather | solution.py:127
  83.7 1.3 convolution_bitcast_fusion.23
  85.0 1.3 convolution_bitcast_fusion.29
  86.2 1.3 convolution_bitcast_fusion.31
  87.5 1.3 convolution_bitcast_fusion.24
  88.8 1.3 convolution_bitcast_fusion.27
  90.0 1.3 convolution_bitcast_fusion.30
  99.9 1.3 fusion.26
  101.2 1.2 convolution_bitcast_fusion.26
  102.7 1.9 multiply_convert_fusion.1
  104.7 0.9 fusion.106
  105.6 1.7 fusion.440
  107.9 1.7 convolution_bitcast_fusion.2
  109.6 1.6 convolution_bitcast_fusion.5
  111.2 1.6 convolution_bitcast_fusion.7
  112.9 1.6 convolution_bitcast_fusion.8
  114.5 1.7 convolution_bitcast_fusion.3
  116.2 1.9 convolution_bitcast_fusion.6
  118.1 1.6 convolution_bitcast_fusion.9
  119.7 1.7 convolution_bitcast_fusion
  121.4 1.4 convolution_bitcast_fusion.4
  123.6 0.9 fusion.104
  124.5 0.9 fusion.103
  126.3 0.9 fusion.101
  127.2 0.9 fusion.100
  129.0 0.9 fusion.98
  129.9 0.9 fusion.97
  131.6 0.9 fusion.95
  132.5 0.9 fusion.94
  134.3 0.9 fusion.92
  135.2 0.9 fusion.91
  137.0 0.9 fusion.89
  137.8 0.9 fusion.88
  139.6 0.9 fusion.86
  140.5 0.9 fusion.85
  142.3 0.9 fusion.83
  143.2 0.9 fusion.82
  144.9 0.9 fusion.80
  145.9 1.9 convolution_add_fusion.14
  157.9 2.1 fusion.12
  160.0 60.2 %all-reduce.11.cloned.1.call-done = f32[27,128,8]{1,2,0:T(8,128)} async-done(((f32[27,128,8]{1,2,0:T(8,128)}), f32[27,128,8]{1,2,0:T(8,128)}) %all-reduce.11.cloned.1.call-update) | async-done | bytes 110608 | tf_op jit(solution)/shard_map/psum | solution.py:149
  220.2 1.6 broadcast_multiply_fusion.1
  221.8 161.0 %reduce-scatter.2.cloned.1.call-done = f32[1,1,128,64]{2,3,0,1:T(8,128)} async-done(((f32[32,1,128,64]{2,3,0,1:T(8,128)}), f32[1,1,128,64]{2,3,0,1:T(8,128)}) %reduce-scatter.2.cloned.1.call-update) | async-done | bytes 32784 | tf_op jit(solution)/shard_map/reduce_scatter | solution.py:141
  383.7 1.0 fusion.79
  385.4 1.0 fusion.78
  386.6 1.0 fusion.76
  387.6 1.0 fusion.75
  388.8 1.0 fusion.73
  389.8 1.0 fusion.72
  393.9 2.2 collective-permute-start.2
  396.1 1.3 collective-permute-start.3
  397.5 0.9 copy-done.14
  398.5 2.8 collective-permute-done.3
  408.7 254.2 %all-reduce.9.cloned.1.call-done = f32[27,64,128]{2,1,0:T(8,128)} async-done(((f32[27,64,128]{2,1,0:T(8,128)}), f32[27,64,128]{2,1,0:T(8,128)}) %all-reduce.9.cloned.1.call-update) | async-done | bytes 884752 | tf_op jit(solution)/shard_map/psum | solution.py:157
  662.9 2.2 broadcast_multiply_fusion
  (283 shorter events, 50.3 us)
Async XLA Ops:
  8.0 73.2 %copy-start = (bf16[27,128,256]{2,1,0:T(8,128)(2,1)S(1)}, bf16[27,128,256]{2,1,0:T(8,128)(2,1)}, u32[]{:S(2)}) copy-start(bf16[27,128,256]{2,1,0:T(8,128)(2,1)} %param.6) | copy-start | bytes 5308420
  9.1 21.3 %collective-permute-start = (bf16[1,64,1,256]{3,2,1,0:T(2,128)(2,1)S(1)}, bf16[1,64,1,256]{3,2,1,0:T(2,128)(2,1)S(1)}, u32[]{:S(2)}, u32[]{:S(2)}) collective-permute-start(bf16[1,64,1,256]{3,2,1,0:T(2,128)(2,1)S(1)} %get-tuple-element.50), channel_id=1, source_target_pairs={{0,1},{1,2},{2,3},{3,4},{4,5},{5,6},{6,7},{7,8},{8,9},{9,10},{10,1... | collective-permute-start | bytes 98312 | tf_op jit(solution)/shard_map/ppermute | solution.py:18
  13.1 17.4 %collective-permute-start.1 = (bf16[1,64,1,256]{3,2,1,0:T(2,128)(2,1)S(1)}, bf16[1,64,1,256]{3,2,1,0:T(2,128)(2,1)S(1)}, u32[]{:S(2)}, u32[]{:S(2)}) collective-permute-start(bf16[1,64,1,256]{3,2,1,0:T(2,128)(2,1)S(1)} %get-tuple-element.51), channel_id=1, source_target_pairs={{1,0},{2,1},{3,2},{4,3},{5,4},{6,5},{7,6},{8,7},{9,8},{10,9},{11,1... | collective-permute-start | bytes 98312 | tf_op jit(solution)/shard_map/ppermute | solution.py:19
  17.5 84.9 %all-to-all-start = ((bf16[32,2,256]{2,1,0:T(2,128)(2,1)}), bf16[32,2,256]{2,1,0:T(2,128)(2,1)S(1)}, u32[]{:S(2)}, u32[]{:S(2)}) async-start(bf16[32,2,256]{2,1,0:T(2,128)(2,1)} %reshape.962), calls=%async_computation | async-start | bytes 65536 | tf_op jit(solution)/shard_map/all_to_all | solution.py:134
  30.3 189.9 %all-reduce.11.cloned.1.call-start = ((), (), s32[]{:S(2)}) async-start(), calls=%async_computation.4 | async-start | bytes 221184 | tf_op jit(solution)/shard_map/psum | solution.py:149
  30.4 4.2 copy-start.67
  30.4 6.6 copy-start.63
  30.4 4.2 copy-start.65
  30.5 4.3 copy-start.15
  33.0 3.1 copy-start.39
  33.0 3.3 copy-start.41
  33.0 3.5 copy-start.43
  33.0 3.8 copy-start.49
  33.0 4.9 copy-start.33
  33.1 5.6 copy-start.27
  33.1 6.3 copy-start.23
  33.1 7.0 %copy-start.17 = (bf16[64,2,256]{2,1,0:T(2,128)(2,1)}, bf16[64,2,256]{2,1,0:T(2,128)(2,1)S(1)}, u32[]{:S(2)}) copy-start(bf16[64,2,256]{2,1,0:T(2,128)(2,1)S(1)} %get-tuple-element.31) | copy-start | bytes 196612
  34.6 2.8 copy-start.45
  34.6 2.8 copy-start.47
  34.6 2.8 copy-start.51
  34.7 2.8 copy-start.53
  34.7 2.8 copy-start.55
  34.7 2.8 copy-start.59
  34.7 3.0 copy-start.38
  34.7 3.5 copy-start.37
  34.7 4.2 copy-start.36
  34.7 4.9 copy-start.31
  34.7 5.1 copy-start.29
  34.7 5.5 copy-start.35
  34.7 5.5 copy-start.25
  34.8 6.2 copy-start.21
  34.8 6.4 copy-start.19
  37.5 3.0 copy-start.57
  81.2 23.5 %copy-start.10 = (bf16[1,128,34,64]{1,3,0,2:T(8,128)(2,1)}, bf16[1,128,34,64]{1,3,0,2:T(8,128)(2,1)S(1)}, u32[]{:S(2)}) copy-start(bf16[1,128,34,64]{1,3,0,2:T(8,128)(2,1)S(1)} %pad.27) | copy-start | bytes 1671172
  118.0 4.7 copy-start.11
  145.8 236.9 %reduce-scatter.2.cloned.1.call-start = ((), (), s32[]{:S(2)}) async-start(), calls=%async_computation.2 | async-start | bytes 1081344 | tf_op jit(solution)/shard_map/reduce_scatter | solution.py:141
  153.5 3.2 copy-start.9
  157.9 225.7 %copy-start.12 = (f32[1,128,2,256]{1,3,2,0:T(8,128)S(1)}, f32[1,128,2,256]{1,3,2,0:T(8,128)}, u32[]{:S(2)}) copy-start(f32[1,128,2,256]{1,3,2,0:T(8,128)} %get-tuple-element.53) | copy-start | bytes 786436
  159.9 226.4 %copy-start.34 = (bf16[64,2,256]{2,1,0:T(2,128)(2,1)S(1)}, bf16[64,2,256]{2,1,0:T(2,128)(2,1)}, u32[]{:S(2)}) copy-start(bf16[64,2,256]{2,1,0:T(2,128)(2,1)} %copy-done.33) | copy-start | bytes 196612
  159.9 228.7 %copy-start.28 = (bf16[64,2,256]{2,1,0:T(2,128)(2,1)S(1)}, bf16[64,2,256]{2,1,0:T(2,128)(2,1)}, u32[]{:S(2)}) copy-start(bf16[64,2,256]{2,1,0:T(2,128)(2,1)} %copy-done.27) | copy-start | bytes 196612
  160.0 230.9 %copy-start.24 = (bf16[64,2,256]{2,1,0:T(2,128)(2,1)S(1)}, bf16[64,2,256]{2,1,0:T(2,128)(2,1)}, u32[]{:S(2)}) copy-start(bf16[64,2,256]{2,1,0:T(2,128)(2,1)} %copy-done.23) | copy-start | bytes 196612
  160.0 231.1 %copy-start.32 = (bf16[64,2,256]{2,1,0:T(2,128)(2,1)S(1)}, bf16[64,2,256]{2,1,0:T(2,128)(2,1)}, u32[]{:S(2)}) copy-start(bf16[64,2,256]{2,1,0:T(2,128)(2,1)} %copy-done.31) | copy-start | bytes 196612
  160.0 231.2 %copy-start.30 = (bf16[64,2,256]{2,1,0:T(2,128)(2,1)S(1)}, bf16[64,2,256]{2,1,0:T(2,128)(2,1)}, u32[]{:S(2)}) copy-start(bf16[64,2,256]{2,1,0:T(2,128)(2,1)} %copy-done.29) | copy-start | bytes 196612
  160.0 502.9 %all-reduce.9.cloned.1.call-start = ((), (), s32[]{:S(2)}) async-start(), calls=%async_computation.3 | async-start | bytes 1769472 | tf_op jit(solution)/shard_map/psum | solution.py:157
  221.8 169.6 %copy-start.18 = (bf16[64,2,256]{2,1,0:T(2,128)(2,1)S(1)}, bf16[64,2,256]{2,1,0:T(2,128)(2,1)}, u32[]{:S(2)}) copy-start(bf16[64,2,256]{2,1,0:T(2,128)(2,1)} %copy-done.17) | copy-start | bytes 196612
  383.5 8.0 %copy-start.26 = (bf16[64,2,256]{2,1,0:T(2,128)(2,1)S(1)}, bf16[64,2,256]{2,1,0:T(2,128)(2,1)}, u32[]{:S(2)}) copy-start(bf16[64,2,256]{2,1,0:T(2,128)(2,1)} %copy-done.25) | copy-start | bytes 196612
  383.6 8.2 %copy-start.58 = (bf16[64,2,256]{2,1,0:T(2,128)(2,1)S(1)}, bf16[64,2,256]{2,1,0:T(2,128)(2,1)}, u32[]{:S(2)}) copy-start(bf16[64,2,256]{2,1,0:T(2,128)(2,1)} %copy-done.57) | copy-start | bytes 196612
  384.7 7.4 %copy-start.22 = (bf16[64,2,256]{2,1,0:T(2,128)(2,1)S(1)}, bf16[64,2,256]{2,1,0:T(2,128)(2,1)}, u32[]{:S(2)}) copy-start(bf16[64,2,256]{2,1,0:T(2,128)(2,1)} %copy-done.21) | copy-start | bytes 196612
  385.4 6.8 %copy-start.20 = (bf16[64,2,256]{2,1,0:T(2,128)(2,1)S(1)}, bf16[64,2,256]{2,1,0:T(2,128)(2,1)}, u32[]{:S(2)}) copy-start(bf16[64,2,256]{2,1,0:T(2,128)(2,1)} %copy-done.19) | copy-start | bytes 196612
  386.4 6.0 copy-start.50
  386.5 6.0 copy-start.56
  387.6 5.1 copy-start.54
  388.6 4.3 copy-start.44
  388.8 4.2 copy-start.52
  389.8 3.4 copy-start.62
  390.9 2.5 copy-start.42
  391.0 2.5 copy-start.48
  391.4 6.0 copy-start.40
  392.5 8.8 %copy-start.16 = (bf16[27,64,128]{2,1,0:T(8,128)(2,1)S(1)}, bf16[27,64,128]{2,1,0:T(8,128)(2,1)}, u32[]{:S(2)}) copy-start(bf16[27,64,128]{2,1,0:T(8,128)(2,1)} %param.5) | copy-start | bytes 1327108
  392.5 8.8 %copy-start.68 = (bf16[256]{0:T(256)(128)(2,1)S(1)}, bf16[256]{0:T(256)(128)(2,1)}, u32[]{:S(2)}) copy-start(bf16[256]{0:T(256)(128)(2,1)} %copy-done.67) | copy-start | bytes 1540
  393.2 8.7 %copy-start.64 = (bf16[256]{0:T(256)(128)(2,1)S(1)}, bf16[256]{0:T(256)(128)(2,1)}, u32[]{:S(2)}) copy-start(bf16[256]{0:T(256)(128)(2,1)} %copy-done.63) | copy-start | bytes 1540
  393.7 8.6 %copy-start.66 = (bf16[256]{0:T(256)(128)(2,1)S(1)}, bf16[256]{0:T(256)(128)(2,1)}, u32[]{:S(2)}) copy-start(bf16[256]{0:T(256)(128)(2,1)} %copy-done.65) | copy-start | bytes 1540
  393.9 4.6 collective-permute-start.2
  396.1 5.2 collective-permute-start.3
  (13 other events, 25.9 us)
Sparse Core Ops, SparseCore 0:
  146.0 74.2 all-reduce.10
Sparse Core Ops, SparseCore 1:
  160.0 222.6 reduce-scatter.1
  398.6 264.3 all-reduce.8
where the time goes:
time: 680 us; the launch traced here: 673 us
  waiting for transfers between devices  478 us (70%)
  matrix products  99.3 us (15%)
  blocking collectives  38.8 us (6%)
  starting transfers between devices  21.6 us (3%)
  between operations  17.5 us (3%)
  other arithmetic  10.4 us (2%)
  local copies, waits for them, and re-layouts  7.13 us (1%)
    psum x1, waiting for transfers between devices, body(): grad_kernel_a = lax.psum(part_a, ('dp', 'space')) * scale_a  254 us
    reduce_scatter x1, waiting for transfers between devices, body(): lax.psum_scatter(jnp.transpose(term_rows, (2, 0, 1, 3)), 'space', scatter...  161 us
    psum x1, waiting for transfers between devices, body(): grad_kernel_b = lax.psum(part_b, 'dp') * scale_b  60.2 us
    all_gather x1, blocking collectives, body(): gathered = lax.all_gather(pooled, 'space', axis=2, tiled=True)  38.8 us
    dot_general x54, matrix products, conv_transposed(): jnp.einsum('io,soxn->sixn', kernel[tap_index], shifted, preferred_element...  36.3 us
    dot_general x54, matrix products, kernel_grad(): jnp.einsum('sixn,soxn->io', shifted, gradient, preferred_element_type=jnp...  33.3 us
    dot_general x54, matrix products, conv_forward(): jnp.einsum('io,sixn->soxn', kernel[tap_index], shifted, preferred_element...  29.7 us
  transfers between devices with their start and end apart: 8, of which 4 were waited for; matrix products, arithmetic and copies ran while one was open for 8% of the time, Pallas kernels for 0%

commit v1 on v0

--- a/solution.py
+++ b/solution.py
@@ -124,7 +124,9 @@
     )
     pooled = pooled.reshape(samples, filters_a, half_planes, half_y * half_z).astype(jnp.bfloat16)
     per_device = kernel_b.shape[2] // lax.axis_size("space")
-    gathered = lax.all_gather(pooled, "space", axis=2, tiled=True)
+    gathered = jnp.concatenate(
+        lax.all_to_all(jnp.stack([pooled] * lax.axis_size("space")), "space", 0, 0), axis=2
+    )
     full_planes = gathered.shape[2]
     own_kernel = lax.dynamic_slice_in_dim(
         kernel_b, lax.axis_index("space") * per_device, per_device, 2

time: 680 us -> 647 us (0.951)
  blocking collectives: 38.8 us -> 0 us
  starting transfers between devices: 21.6 us -> 31.6 us
    all_gather x1 -> x0, blocking collectives: 38.8 us -> none  [body(): gathered = lax.all_gather(pooled, 'space', axis=2, tiled=True)]
    all_to_all x0 -> x1, waiting for transfers between devices: none -> 14.2 us  [body(): lax.all_to_all(jnp.stack([pooled] * lax.axis_size('space')), 'space', 0, 0)]
    psum x1, waiting for transfers between devices: 60.2 us -> 48.3 us  [body(): grad_kernel_b = lax.psum(part_b, 'dp') * scale_b]
    all_to_all x0 -> x1, starting transfers between devices: none -> 9.22 us  [body(): lax.all_to_all(jnp.stack([pooled] * lax.axis_size('space')), 'space', 0, 0)]
  transfers between devices with their start and end apart: 8 -> 9, of which waited for: 4 -> 5; matrix products, arithmetic and copies ran while one was open for 8% -> 6% of each run, Pallas kernels for 0% -> 0%
where the time goes in v1:
time: 647 us; the launch traced here: 640 us
  waiting for transfers between devices  480 us (74%)
  matrix products  92.7 us (14%)
  starting transfers between devices  31.6 us (5%)
  between operations  17.4 us (3%)
  other arithmetic  10.4 us (2%)
  local copies, waits for them, and re-layouts  8.05 us (1%)
    psum x1, waiting for transfers between devices, body(): grad_kernel_a = lax.psum(part_a, ('dp', 'space')) * scale_a  254 us
    reduce_scatter x1, waiting for transfers between devices, body(): lax.psum_scatter(jnp.transpose(term_rows, (2, 0, 1, 3)), 'space', scatter...  161 us
    psum x1, waiting for transfers between devices, body(): grad_kernel_b = lax.psum(part_b, 'dp') * scale_b  48.3 us
    dot_general x54, matrix products, conv_transposed(): jnp.einsum('io,soxn->sixn', kernel[tap_index], shifted, preferred_element...  36.3 us
    dot_general x54, matrix products, kernel_grad(): jnp.einsum('sixn,soxn->io', shifted, gradient, preferred_element_type=jnp...  33.2 us
    dot_general x54, matrix products, conv_forward(): jnp.einsum('io,sixn->soxn', kernel[tap_index], shifted, preferred_element...  23.2 us
    all_to_all x1, waiting for transfers between devices, body(): lax.all_to_all(jnp.stack([pooled] * lax.axis_size('space')), 'space', 0, 0)  14.2 us
  transfers between devices with their start and end apart: 9, of which 5 were waited for; matrix products, arithmetic and copies ran while one was open for 6% of the time, Pallas kernels for 0%

profile of v1, /device:TPU:1, one launch (start us, length us, event | category | flops | bytes accessed | tf_op | source)
XLA Modules:
  0.0 640.4 jit_solution(14732429816514827848)
XLA Ops:
  8.0 1.1 fusion.847
  9.1 3.9 collective-permute-start
  13.1 1.3 collective-permute-start.1
  14.4 0.9 copy.229
  15.8 1.0 reduce.3
  17.5 12.8 %all-to-all-start = ((bf16[32,2,256]{2,1,0:T(2,128)(2,1)}), bf16[32,2,256]{2,1,0:T(2,128)(2,1)S(1)}, u32[]{:S(2)}, u32[]{:S(2)}) async-start(bf16[32,2,256]{2,1,0:T(2,128)(2,1)} %reshape.972), calls=%async_computation | async-start | bytes 65536 | tf_op jit(solution)/shard_map/all_to_all | solution.py:136
  30.4 1.5 select_maximum_fusion
  31.9 1.0 fusion.370
  33.0 1.5 fusion.368
  41.1 1.0 multiply_reduce_fusion
  42.3 0.9 stack.203
  43.2 9.2 %all-to-all-start.1 = ((bf16[32,1,128,1,64]{2,4,3,1,0:T(8,128)(2,1)}), bf16[32,1,128,1,64]{2,4,3,1,0:T(8,128)(2,1)S(1)}, u32[]{:S(2)}, u32[]{:S(2)}) async-start(bf16[32,1,128,1,64]{2,4,3,1,0:T(8,128)(2,1)} %stack.203), calls=%async_computation.1 | async-start | bytes 1048576 | tf_op jit(solution)/shard_map/all_to_all | solution.py:128
  53.2 14.2 %all-to-all-done.1 = bf16[32,1,128,1,64]{2,4,3,1,0:T(8,128)(2,1)S(1)} async-done(((bf16[32,1,128,1,64]{2,4,3,1,0:T(8,128)(2,1)}), bf16[32,1,128,1,64]{2,4,3,1,0:T(8,128)(2,1)S(1)}, u32[]{:S(2)}, u32[]{:S(2)}) %all-to-all-start.1) | async-done | bytes 524320 | tf_op jit(solution)/shard_map/all_to_all | solution.py:128
  84.1 0.9 fusion.106
  85.0 1.7 fusion.437
  87.4 1.7 convolution_bitcast_fusion.2
  89.0 1.6 convolution_bitcast_fusion.5
  90.7 1.6 convolution_bitcast_fusion.7
  92.3 1.6 convolution_bitcast_fusion.8
  93.9 1.7 convolution_bitcast_fusion.3
  95.6 1.7 convolution_bitcast_fusion.6
  97.3 1.6 convolution_bitcast_fusion.9
  98.9 1.9 convolution_bitcast_fusion
  100.8 1.4 convolution_bitcast_fusion.4
  102.2 0.9 fusion.105
  103.0 0.9 fusion.104
  103.9 0.9 fusion.103
  105.7 0.9 fusion.101
  106.6 0.9 fusion.100
  107.5 0.9 fusion.99
  108.4 0.9 fusion.98
  109.2 0.9 fusion.97
  110.1 0.9 fusion.96
  111.0 0.9 fusion.95
  111.9 0.9 fusion.94
  113.7 0.9 fusion.92
  114.6 0.9 fusion.91
  115.5 0.9 fusion.90
  116.3 0.9 fusion.89
  117.2 0.9 fusion.88
  118.1 0.9 fusion.87
  119.0 0.9 fusion.86
  119.9 0.9 fusion.85
  121.6 0.9 fusion.83
  122.5 0.9 fusion.82
  123.4 0.9 fusion.81
  124.3 0.9 fusion.80
  125.3 1.9 convolution_add_fusion.14
  137.2 2.1 fusion.12
  139.6 48.3 %all-reduce.11.cloned.1.call-done = f32[27,128,8]{1,2,0:T(8,128)} async-done(((f32[27,128,8]{1,2,0:T(8,128)}), f32[27,128,8]{1,2,0:T(8,128)}) %all-reduce.11.cloned.1.call-update) | async-done | bytes 110608 | tf_op jit(solution)/shard_map/psum | solution.py:151
  188.0 1.6 broadcast_multiply_fusion.1
  189.5 160.8 %reduce-scatter.2.cloned.1.call-done = f32[1,1,128,64]{2,3,0,1:T(8,128)} async-done(((f32[32,1,128,64]{2,3,0,1:T(8,128)}), f32[1,1,128,64]{2,3,0,1:T(8,128)}) %reduce-scatter.2.cloned.1.call-update) | async-done | bytes 32784 | tf_op jit(solution)/shard_map/reduce_scatter | solution.py:143
  351.3 1.0 fusion.79
  352.9 1.0 fusion.78
  354.1 1.0 fusion.76
  355.2 1.0 fusion.75
  356.4 1.0 fusion.73
  357.4 1.0 fusion.72
  361.5 2.3 collective-permute-start.2
  363.7 1.3 collective-permute-start.3
  365.2 0.9 copy-done.12
  366.2 2.8 collective-permute-done.3
  376.4 254.1 %all-reduce.9.cloned.1.call-done = f32[27,64,128]{2,1,0:T(8,128)} async-done(((f32[27,64,128]{2,1,0:T(8,128)}), f32[27,64,128]{2,1,0:T(8,128)}) %all-reduce.9.cloned.1.call-update) | async-done | bytes 884752 | tf_op jit(solution)/shard_map/psum | solution.py:159
  630.5 2.2 broadcast_multiply_fusion
  (281 shorter events, 50.5 us)
Async XLA Ops:
  8.0 59.5 %copy-start = (bf16[27,128,256]{2,1,0:T(8,128)(2,1)S(1)}, bf16[27,128,256]{2,1,0:T(8,128)(2,1)}, u32[]{:S(2)}) copy-start(bf16[27,128,256]{2,1,0:T(8,128)(2,1)} %param.6) | copy-start | bytes 5308420
  9.1 21.3 %collective-permute-start = (bf16[1,64,1,256]{3,2,1,0:T(2,128)(2,1)S(1)}, bf16[1,64,1,256]{3,2,1,0:T(2,128)(2,1)S(1)}, u32[]{:S(2)}, u32[]{:S(2)}) collective-permute-start(bf16[1,64,1,256]{3,2,1,0:T(2,128)(2,1)S(1)} %get-tuple-element.50), channel_id=1, source_target_pairs={{0,1},{1,2},{2,3},{3,4},{4,5},{5,6},{6,7},{7,8},{8,9},{9,10},{10,1... | collective-permute-start | bytes 98312 | tf_op jit(solution)/shard_map/ppermute | solution.py:18
  13.1 17.3 %collective-permute-start.1 = (bf16[1,64,1,256]{3,2,1,0:T(2,128)(2,1)S(1)}, bf16[1,64,1,256]{3,2,1,0:T(2,128)(2,1)S(1)}, u32[]{:S(2)}, u32[]{:S(2)}) collective-permute-start(bf16[1,64,1,256]{3,2,1,0:T(2,128)(2,1)S(1)} %get-tuple-element.51), channel_id=1, source_target_pairs={{1,0},{2,1},{3,2},{4,3},{5,4},{6,5},{7,6},{8,7},{9,8},{10,9},{11,1... | collective-permute-start | bytes 98312 | tf_op jit(solution)/shard_map/ppermute | solution.py:19
  17.5 24.7 %all-to-all-start = ((bf16[32,2,256]{2,1,0:T(2,128)(2,1)}), bf16[32,2,256]{2,1,0:T(2,128)(2,1)S(1)}, u32[]{:S(2)}, u32[]{:S(2)}) async-start(bf16[32,2,256]{2,1,0:T(2,128)(2,1)} %reshape.972), calls=%async_computation | async-start | bytes 65536 | tf_op jit(solution)/shard_map/all_to_all | solution.py:136
  30.3 2.6 copy-start.65
  30.3 6.6 %copy-start.61 = (bf16[256]{0:T(256)(128)(2,1)}, bf16[256]{0:T(256)(128)(2,1)S(1)}, u32[]{:S(2)}) copy-start(bf16[256]{0:T(256)(128)(2,1)S(1)} %get-tuple-element.57) | copy-start | bytes 1540
  30.4 4.2 copy-start.63
  30.4 4.3 copy-start.13
  32.9 3.1 copy-start.37
  32.9 3.3 copy-start.39
  32.9 3.5 copy-start.41
  33.0 3.7 copy-start.47
  33.0 4.9 copy-start.31
  33.0 5.6 copy-start.25
  33.0 6.3 copy-start.21
  33.0 6.9 %copy-start.15 = (bf16[64,2,256]{2,1,0:T(2,128)(2,1)}, bf16[64,2,256]{2,1,0:T(2,128)(2,1)S(1)}, u32[]{:S(2)}) copy-start(bf16[64,2,256]{2,1,0:T(2,128)(2,1)S(1)} %get-tuple-element.31) | copy-start | bytes 196612
  34.5 2.8 copy-start.43
  34.5 2.8 copy-start.45
  34.6 2.8 copy-start.49
  34.6 2.8 copy-start.51
  34.6 2.8 copy-start.53
  34.6 2.8 copy-start.57
  34.6 3.0 copy-start.36
  34.6 3.5 copy-start.35
  34.6 4.2 copy-start.34
  34.6 4.9 copy-start.29
  34.6 5.1 copy-start.27
  34.7 5.5 copy-start.33
  34.7 5.5 copy-start.23
  34.7 6.2 copy-start.19
  34.7 6.4 %copy-start.17 = (bf16[64,2,256]{2,1,0:T(2,128)(2,1)}, bf16[64,2,256]{2,1,0:T(2,128)(2,1)S(1)}, u32[]{:S(2)}) copy-start(bf16[64,2,256]{2,1,0:T(2,128)(2,1)S(1)} %get-tuple-element.12) | copy-start | bytes 196612
  37.4 3.0 copy-start.55
  43.2 24.2 %all-to-all-start.1 = ((bf16[32,1,128,1,64]{2,4,3,1,0:T(8,128)(2,1)}), bf16[32,1,128,1,64]{2,4,3,1,0:T(8,128)(2,1)S(1)}, u32[]{:S(2)}, u32[]{:S(2)}) async-start(bf16[32,1,128,1,64]{2,4,3,1,0:T(8,128)(2,1)} %stack.203), calls=%async_computation.1 | async-start | bytes 1048576 | tf_op jit(solution)/shard_map/all_to_all | solution.py:128
  52.4 135.6 %all-reduce.11.cloned.1.call-start = ((), (), s32[]{:S(2)}) async-start(), calls=%async_computation.5 | async-start | bytes 221184 | tf_op jit(solution)/shard_map/psum | solution.py:151
  125.2 225.1 %reduce-scatter.2.cloned.1.call-start = ((), (), s32[]{:S(2)}) async-start(), calls=%async_computation.3 | async-start | bytes 1081344 | tf_op jit(solution)/shard_map/reduce_scatter | solution.py:143
  132.9 3.2 copy-start.9
  134.7 2.5 copy-start.4
  137.2 213.9 %copy-start.10 = (f32[1,128,2,256]{1,3,2,0:T(8,128)S(1)}, f32[1,128,2,256]{1,3,2,0:T(8,128)}, u32[]{:S(2)}) copy-start(f32[1,128,2,256]{1,3,2,0:T(8,128)} %get-tuple-element.53) | copy-start | bytes 786436
  139.3 214.7 %copy-start.32 = (bf16[64,2,256]{2,1,0:T(2,128)(2,1)S(1)}, bf16[64,2,256]{2,1,0:T(2,128)(2,1)}, u32[]{:S(2)}) copy-start(bf16[64,2,256]{2,1,0:T(2,128)(2,1)} %copy-done.31) | copy-start | bytes 196612
  139.3 216.9 %copy-start.26 = (bf16[64,2,256]{2,1,0:T(2,128)(2,1)S(1)}, bf16[64,2,256]{2,1,0:T(2,128)(2,1)}, u32[]{:S(2)}) copy-start(bf16[64,2,256]{2,1,0:T(2,128)(2,1)} %copy-done.25) | copy-start | bytes 196612
  139.3 219.1 %copy-start.22 = (bf16[64,2,256]{2,1,0:T(2,128)(2,1)S(1)}, bf16[64,2,256]{2,1,0:T(2,128)(2,1)}, u32[]{:S(2)}) copy-start(bf16[64,2,256]{2,1,0:T(2,128)(2,1)} %copy-done.21) | copy-start | bytes 196612
  139.3 219.3 %copy-start.30 = (bf16[64,2,256]{2,1,0:T(2,128)(2,1)S(1)}, bf16[64,2,256]{2,1,0:T(2,128)(2,1)}, u32[]{:S(2)}) copy-start(bf16[64,2,256]{2,1,0:T(2,128)(2,1)} %copy-done.29) | copy-start | bytes 196612
  139.4 219.4 %copy-start.28 = (bf16[64,2,256]{2,1,0:T(2,128)(2,1)S(1)}, bf16[64,2,256]{2,1,0:T(2,128)(2,1)}, u32[]{:S(2)}) copy-start(bf16[64,2,256]{2,1,0:T(2,128)(2,1)} %copy-done.27) | copy-start | bytes 196612
  139.4 491.1 %all-reduce.9.cloned.1.call-start = ((), (), s32[]{:S(2)}) async-start(), calls=%async_computation.4 | async-start | bytes 1769472 | tf_op jit(solution)/shard_map/psum | solution.py:159
  189.5 169.4 %copy-start.16 = (bf16[64,2,256]{2,1,0:T(2,128)(2,1)S(1)}, bf16[64,2,256]{2,1,0:T(2,128)(2,1)}, u32[]{:S(2)}) copy-start(bf16[64,2,256]{2,1,0:T(2,128)(2,1)} %copy-done.15) | copy-start | bytes 196612
  351.1 8.0 %copy-start.24 = (bf16[64,2,256]{2,1,0:T(2,128)(2,1)S(1)}, bf16[64,2,256]{2,1,0:T(2,128)(2,1)}, u32[]{:S(2)}) copy-start(bf16[64,2,256]{2,1,0:T(2,128)(2,1)} %copy-done.23) | copy-start | bytes 196612
  351.1 8.2 %copy-start.56 = (bf16[64,2,256]{2,1,0:T(2,128)(2,1)S(1)}, bf16[64,2,256]{2,1,0:T(2,128)(2,1)}, u32[]{:S(2)}) copy-start(bf16[64,2,256]{2,1,0:T(2,128)(2,1)} %copy-done.55) | copy-start | bytes 196612
  352.3 7.4 %copy-start.20 = (bf16[64,2,256]{2,1,0:T(2,128)(2,1)S(1)}, bf16[64,2,256]{2,1,0:T(2,128)(2,1)}, u32[]{:S(2)}) copy-start(bf16[64,2,256]{2,1,0:T(2,128)(2,1)} %copy-done.19) | copy-start | bytes 196612
  352.9 6.8 %copy-start.18 = (bf16[64,2,256]{2,1,0:T(2,128)(2,1)S(1)}, bf16[64,2,256]{2,1,0:T(2,128)(2,1)}, u32[]{:S(2)}) copy-start(bf16[64,2,256]{2,1,0:T(2,128)(2,1)} %copy-done.17) | copy-start | bytes 196612
  354.0 6.0 copy-start.48
  354.1 6.0 copy-start.54
  355.2 5.1 copy-start.52
  356.2 4.3 copy-start.42
  356.4 4.3 copy-start.50
  357.4 3.4 copy-start.60
  358.5 2.5 copy-start.40
  358.6 2.5 copy-start.46
  359.0 6.1 copy-start.38
  360.1 8.9 %copy-start.14 = (bf16[27,64,128]{2,1,0:T(8,128)(2,1)S(1)}, bf16[27,64,128]{2,1,0:T(8,128)(2,1)}, u32[]{:S(2)}) copy-start(bf16[27,64,128]{2,1,0:T(8,128)(2,1)} %param.5) | copy-start | bytes 1327108
  360.1 8.9 %copy-start.66 = (bf16[256]{0:T(256)(128)(2,1)S(1)}, bf16[256]{0:T(256)(128)(2,1)}, u32[]{:S(2)}) copy-start(bf16[256]{0:T(256)(128)(2,1)} %copy-done.65) | copy-start | bytes 1540
  360.8 8.7 %copy-start.62 = (bf16[256]{0:T(256)(128)(2,1)S(1)}, bf16[256]{0:T(256)(128)(2,1)}, u32[]{:S(2)}) copy-start(bf16[256]{0:T(256)(128)(2,1)} %copy-done.61) | copy-start | bytes 1540
  361.3 8.7 %copy-start.64 = (bf16[256]{0:T(256)(128)(2,1)S(1)}, bf16[256]{0:T(256)(128)(2,1)}, u32[]{:S(2)}) copy-start(bf16[256]{0:T(256)(128)(2,1)} %copy-done.63) | copy-start | bytes 1540
  361.5 4.7 collective-permute-start.2
  363.7 5.2 collective-permute-start.3
  (12 other events, 23.4 us)
Sparse Core Ops, SparseCore 0:
  125.3 62.5 all-reduce.10
Sparse Core Ops, SparseCore 1:
  139.4 210.8 reduce-scatter.1
  366.2 264.2 all-reduce.8
